TPU v7x, 32 devices: a whole 2x2x4 slice. The times are simulated.
32 devices in a mesh: lat: 8 (over y, x, core), lon: 4 (over z).
Axes of the slice: x: 2, y: 2, z: 4, core: 2. Of those that a mesh axis runs over, the one named last changes fastest.
Arguments:
- noise: float32 [4, 8, 128, 1024], P(None, None, 'lat', 'lon'), may hold values from -6 to 6
- diff_lat: float32 [8, 128, 1024], P(None, 'lat', 'lon'), may hold values from 0.05 to 0.24
- diff_lon: float32 [8, 128, 1024], P(None, 'lat', 'lon'), may hold values from 0.05 to 0.24
- shear: float32 [8, 128, 1024], P(None, 'lat', 'lon'), may hold values from -0.9 to 0.9
- sea_mask: int32 [8, 128, 1024], P(None, 'lat', 'lon'), may hold values from 0 to 1, as said below
Outputs:
- normalized: float32 [4, 8, 128, 1024], P(None, None, 'lat', 'lon')
- mean_var: float32 [], replicated
Inputs may be any that keep to these rules, and one draw needn't show every extreme that they name: `sea_mask`: every block of 16 latitude rows by 256 longitude columns has its own chance for each cell to be wet, from a quarter to one; the block of the first rows and first columns is wet at every level.
All inputs are finite; a program needn't handle non-finite values.
Results may differ from a plain program's by a relative error of at most 0.0003.
Values sent between devices are 32-bit elements; how exact they have to be, the bound alone decides.
No kernel may reach another device: no remote copies, remote signals or barrier semaphores. Data moves between devices by JAX's collectives and lax.ppermute only.
A program may use at most 64 MiB of HBM per device.

v0:
```python
import jax
import jax.numpy as jnp
from jax import lax
from jax.sharding import PartitionSpec as P

SAMPLES = 4
ITERS = 4


def with_halo(x, sides, width, wrap):
    for axis, dim in sides:
        size, length = (lax.axis_size(axis), x.shape[dim])
        up = [(i, (i + 1) % size) for i in range(size if wrap else size - 1)]
        down = [(j, i) for i, j in up]
        last = lax.slice_in_dim(x, length - width, length, axis=dim)
        first = lax.slice_in_dim(x, 0, width, axis=dim)
        before = lax.ppermute(last, axis, up)
        after = lax.ppermute(first, axis, down)
        x = jnp.concatenate([before, x, after], axis=dim)
    return x


def widen(field, width):
    field = with_halo(field, (("lon", 3),), width, True)
    return with_halo(field, (("lat", 2),), width, False)


def adjoint_step(padded, tensors):
    height = padded.shape[2]
    breadth = padded.shape[3]
    k11 = tensors[0]
    k22 = tensors[1]
    cross = tensors[2] * jnp.sqrt(k11 * k22)
    masked = tensors[3] * padded
    table = [
        ((0, 0), 1.0 - 2.0 * (k11 + k22)),
        ((1, 0), k11),
        ((-1, 0), k11),
        ((0, 1), k22),
        ((0, -1), k22),
        ((1, 1), 0.5 * cross),
        ((-1, -1), 0.5 * cross),
        ((1, -1), -0.5 * cross),
        ((-1, 1), -0.5 * cross),
    ]
    total = jnp.zeros(padded.shape[:2] + (height - 2, breadth - 2), jnp.float32)
    for offset, weight in table:
        product = weight * masked
        total = (
            total
            + product[
                :,
                :,
                1 - offset[0] : height - 1 - offset[0],
                1 - offset[1] : breadth - 1 - offset[1],
            ]
        )
    return total


def shards(noise, diff_lat, diff_lon, shear, sea_mask):
    rows = noise.shape[2]
    cols = noise.shape[3]
    wet = sea_mask.astype(jnp.float32)
    stacked = jnp.stack([diff_lat, diff_lon, shear, wet], axis=0)
    wide_tensors = widen(stacked, ITERS)
    field = noise
    field = widen(field, ITERS)
    for step in range(ITERS):
        reach = ITERS - step
        tensors = wide_tensors[
            :, :, ITERS - reach : ITERS + rows + reach, ITERS - reach : ITERS + cols + reach
        ]
        field = adjoint_step(field, tensors)
    var = jnp.sum(field * field, axis=0) / SAMPLES
    wet_sum, wet_count = lax.psum((jnp.sum(wet * var), jnp.sum(wet)), ("lat", "lon"))
    mean_var = wet_sum / wet_count
    safe = jnp.where(wet > 0, var, 1.0)
    factor = wet * jnp.sqrt(mean_var / (safe + 1e-06))
    return (field * factor, mean_var)


def solution(mesh):
    return jax.shard_map(
        shards,
        mesh=mesh,
        in_specs=(
            P(None, None, "lat", "lon"),
            P(None, "lat", "lon"),
            P(None, "lat", "lon"),
            P(None, "lat", "lon"),
            P(None, "lat", "lon"),
        ),
        out_specs=(P(None, None, "lat", "lon"), P()),
        check_vma=False,
    )
```

profile of v0, /device:TPU:0, one launch (start us, length us, event | category | flops | bytes accessed | tf_op | source)
XLA Modules:
  0.0 102.8 jit_solution(17644934202735698330)
XLA Ops:
  0.6 0.0 copy-start.4
  0.6 0.0 copy-start.3
  0.7 0.0 copy-start.2
  0.7 1.0 convert_bitcast_fusion
  1.6 1.1 %pad_maximum_fusion.1 = f32[4,8,16,256]{3,2,1,0:T(8,128)S(1)} fusion(f32[1,8,16,256]{3,2,1,0:T(8,128)S(1)} %convert_bitcast_fusion, f32[1,8,16,256]{3,2,1,0:T(8,128)} %bitcast.53, f32[1,8,16,256]{3,2,1,0:T(8,128)} %bitcast.56, f32[1,8,16,256]{3,2,1,0:T(8,128)} %bitcast.59), kind=kLoop, calls=%fused_computation.57 | loop fusion | flops 393216 | bytes 1048576 | tf_op jit(solution)/shard_map/stack | solution.py:65
  2.7 0.0 copy-start
  2.7 0.1 fusion.7
  2.9 3.1 %collective-permute-start = (f32[4,8,16,4]{3,2,1,0:T(8,128)S(1)}, f32[4,8,16,4]{3,2,1,0:T(8,128)S(1)}, u32[]{:S(2)}, u32[]{:S(2)}) collective-permute-start(f32[4,8,16,4]{3,2,1,0:T(8,128)S(1)} %get-tuple-element.58), channel_id=1, source_target_pairs={{0,1},{1,2},{2,3},{3,0},{4,5},{5,6},{6,7},{7,4},{8,9},{9,10},{10,1... | collective-permute-start | bytes 24584 | tf_op jit(solution)/shard_map/ppermute | solution.py:17
  6.0 2.1 %collective-permute-start.1 = (f32[4,8,16,4]{3,2,1,0:T(8,128)S(1)}, f32[4,8,16,4]{3,2,1,0:T(8,128)S(1)}, u32[]{:S(2)}, u32[]{:S(2)}) collective-permute-start(f32[4,8,16,4]{3,2,1,0:T(8,128)S(1)} %get-tuple-element.59), channel_id=1, source_target_pairs={{1,0},{2,1},{3,2},{0,3},{5,4},{6,5},{7,6},{4,7},{9,8},{10,9},{11,1... | collective-permute-start | bytes 24584 | tf_op jit(solution)/shard_map/ppermute | solution.py:18
  8.0 7.1 %collective-permute-done = f32[4,8,16,4]{3,2,1,0:T(8,128)S(1)} collective-permute-done((f32[4,8,16,4]{3,2,1,0:T(8,128)S(1)}, f32[4,8,16,4]{3,2,1,0:T(8,128)S(1)}, u32[]{:S(2)}, u32[]{:S(2)}) %collective-permute-start) | collective-permute-done | bytes 8224 | tf_op jit(solution)/shard_map/ppermute | solution.py:17
  15.2 4.2 %collective-permute-done.1 = f32[4,8,16,4]{3,2,1,0:T(8,128)S(1)} collective-permute-done((f32[4,8,16,4]{3,2,1,0:T(8,128)S(1)}, f32[4,8,16,4]{3,2,1,0:T(8,128)S(1)}, u32[]{:S(2)}, u32[]{:S(2)}) %collective-permute-start.1) | collective-permute-done | bytes 8224 | tf_op jit(solution)/shard_map/ppermute | solution.py:18
  19.4 0.3 pad_maximum_fusion.10
  19.7 1.4 %collective-permute-start.2 = (f32[4,8,4,264]{3,2,1,0:T(4,128)S(1)}, f32[4,8,4,264]{3,2,1,0:T(4,128)S(1)}, u32[]{:S(2)}, u32[]{:S(2)}) collective-permute-start(f32[4,8,4,264]{3,2,1,0:T(4,128)S(1)} %get-tuple-element.54), channel_id=1, source_target_pairs={{0,4},{4,8},{8,12},{12,16},{16,20},{20,24},{24,28},{1,5},{5,9},{9,... | collective-permute-start | bytes 405512 | tf_op jit(solution)/shard_map/ppermute | solution.py:17
  21.1 1.3 %collective-permute-start.3 = (f32[4,8,4,264]{3,2,1,0:T(4,128)S(1)}, f32[4,8,4,264]{3,2,1,0:T(4,128)S(1)}, u32[]{:S(2)}, u32[]{:S(2)}) collective-permute-start(f32[4,8,4,264]{3,2,1,0:T(4,128)S(1)} %get-tuple-element.55), channel_id=1, source_target_pairs={{4,0},{8,4},{12,8},{16,12},{20,16},{24,20},{28,24},{5,1},{9,5},{13... | collective-permute-start | bytes 405512 | tf_op jit(solution)/shard_map/ppermute | solution.py:18
  22.4 0.1 fusion.6
  22.5 1.7 %collective-permute-start.4 = (f32[4,8,16,4]{3,2,1,0:T(8,128)S(1)}, f32[4,8,16,4]{3,2,1,0:T(8,128)S(1)}, u32[]{:S(2)}, u32[]{:S(2)}) collective-permute-start(f32[4,8,16,4]{3,2,1,0:T(8,128)S(1)} %get-tuple-element.56), channel_id=1, source_target_pairs={{0,1},{1,2},{2,3},{3,0},{4,5},{5,6},{6,7},{7,4},{8,9},{9,10},{10,1... | collective-permute-start | bytes 24584 | tf_op jit(solution)/shard_map/ppermute | solution.py:17
  24.3 2.1 %collective-permute-start.5 = (f32[4,8,16,4]{3,2,1,0:T(8,128)S(1)}, f32[4,8,16,4]{3,2,1,0:T(8,128)S(1)}, u32[]{:S(2)}, u32[]{:S(2)}) collective-permute-start(f32[4,8,16,4]{3,2,1,0:T(8,128)S(1)} %get-tuple-element.57), channel_id=1, source_target_pairs={{1,0},{2,1},{3,2},{0,3},{5,4},{6,5},{7,6},{4,7},{9,8},{10,9},{11,1... | collective-permute-start | bytes 24584 | tf_op jit(solution)/shard_map/ppermute | solution.py:18
  26.4 5.5 %collective-permute-done.4 = f32[4,8,16,4]{3,2,1,0:T(8,128)S(1)} collective-permute-done((f32[4,8,16,4]{3,2,1,0:T(8,128)S(1)}, f32[4,8,16,4]{3,2,1,0:T(8,128)S(1)}, u32[]{:S(2)}, u32[]{:S(2)}) %collective-permute-start.4) | collective-permute-done | bytes 8224 | tf_op jit(solution)/shard_map/ppermute | solution.py:17
  31.9 7.0 %collective-permute-done.5 = f32[4,8,16,4]{3,2,1,0:T(8,128)S(1)} collective-permute-done((f32[4,8,16,4]{3,2,1,0:T(8,128)S(1)}, f32[4,8,16,4]{3,2,1,0:T(8,128)S(1)}, u32[]{:S(2)}, u32[]{:S(2)}) %collective-permute-start.5) | collective-permute-done | bytes 8224 | tf_op jit(solution)/shard_map/ppermute | solution.py:18
  38.9 0.3 pad_maximum_fusion.4
  39.2 2.0 %collective-permute-start.6 = (f32[4,8,4,264]{3,2,1,0:T(4,128)S(1)}, f32[4,8,4,264]{3,2,1,0:T(4,128)S(1)}, u32[]{:S(2)}, u32[]{:S(2)}) collective-permute-start(f32[4,8,4,264]{3,2,1,0:T(4,128)S(1)} %get-tuple-element.52), channel_id=1, source_target_pairs={{0,4},{4,8},{8,12},{12,16},{16,20},{20,24},{24,28},{1,5},{5,9},{9,... | collective-permute-start | bytes 405512 | tf_op jit(solution)/shard_map/ppermute | solution.py:17
  41.2 1.3 %collective-permute-start.7 = (f32[4,8,4,264]{3,2,1,0:T(4,128)S(1)}, f32[4,8,4,264]{3,2,1,0:T(4,128)S(1)}, u32[]{:S(2)}, u32[]{:S(2)}) collective-permute-start(f32[4,8,4,264]{3,2,1,0:T(4,128)S(1)} %get-tuple-element.53), channel_id=1, source_target_pairs={{4,0},{8,4},{12,8},{16,12},{20,16},{24,20},{28,24},{5,1},{9,5},{13... | collective-permute-start | bytes 405512 | tf_op jit(solution)/shard_map/ppermute | solution.py:18
  42.5 0.0 collective-permute-done.2
  42.5 0.0 collective-permute-done.3
  42.6 0.5 pad_maximum_fusion
  43.1 0.2 subtract_bitcast_fusion
  43.2 0.4 subtract_bitcast_fusion.1
  43.6 0.4 subtract_bitcast_fusion.2
  44.1 0.4 subtract_bitcast_fusion.3
  44.5 0.1 slice.269
  44.6 0.1 slice.280
  44.8 0.1 slice.291
  44.9 0.1 slice.302
  45.0 1.7 %collective-permute-done.7 = f32[4,8,4,264]{3,2,1,0:T(4,128)S(1)} collective-permute-done((f32[4,8,4,264]{3,2,1,0:T(4,128)S(1)}, f32[4,8,4,264]{3,2,1,0:T(4,128)S(1)}, u32[]{:S(2)}, u32[]{:S(2)}) %collective-permute-start.7) | collective-permute-done | bytes 135200 | tf_op jit(solution)/shard_map/ppermute | solution.py:18
  46.7 0.6 broadcast_multiply_fusion.15
  47.3 0.3 broadcast_multiply_fusion.14
  47.7 2.0 %broadcast_multiply_fusion.11 = (f32[4,8,22,262]{3,2,1,0:T(8,128)S(1)}, f32[4,8,22,262]{3,2,1,0:T(8,128)S(1)}) fusion(f32[8,22,262]{2,1,0:T(8,128)S(1)} %get-tuple-element.39, f32[4,8,24,264]{3,2,1,0:T(8,128)S(1)} %get-tuple-element.51, f32[4,8,24,264]{3,2,1,0:T(8,128)S(1)} %get-tuple-element.50, f32[4,8,24,264]{3,2,1,0:T(8,128)S(1)} %get-tuple-element.49, ...), kind=kLoop, calls=%fused_computation.43 | loop fusion | flops 2028928 | bytes 8669056 | tf_op jit(solution)/shard_map/mul | solution.py:48
  49.7 0.3 broadcast_multiply_fusion.10
  50.0 2.0 %broadcast_multiply_fusion.7 = (f32[4,8,20,260]{3,2,1,0:T(8,128)S(1)}, f32[4,8,20,260]{3,2,1,0:T(8,128)S(1)}) fusion(f32[8,20,260]{2,1,0:T(8,128)S(1)} %get-tuple-element.30, f32[4,8,22,262]{3,2,1,0:T(8,128)S(1)} %get-tuple-element.42, f32[4,8,22,262]{3,2,1,0:T(8,128)S(1)} %get-tuple-element.41, f32[4,8,22,262]{3,2,1,0:T(8,128)S(1)} %get-tuple-element.40, ...), kind=kLoop, calls=%fused_computation.39 | loop fusion | flops 1830400 | bytes 7820800 | tf_op jit(solution)/shard_map/mul | solution.py:48
  52.0 0.3 broadcast_multiply_fusion.6
  52.4 2.0 %broadcast_multiply_fusion.3 = (f32[4,8,18,258]{3,2,1,0:T(8,128)S(1)}, f32[4,8,18,258]{3,2,1,0:T(8,128)S(1)}) fusion(f32[8,18,258]{2,1,0:T(8,128)S(1)} %get-tuple-element.21, f32[4,8,20,260]{3,2,1,0:T(8,128)S(1)} %get-tuple-element.33, f32[4,8,20,260]{3,2,1,0:T(8,128)S(1)} %get-tuple-element.32, f32[4,8,20,260]{3,2,1,0:T(8,128)S(1)} %get-tuple-element.31, ...), kind=kLoop, calls=%fused_computation.35 | loop fusion | flops 1634688 | bytes 6984576 | tf_op jit(solution)/shard_map/mul | solution.py:48
  54.4 0.3 broadcast_multiply_fusion.2
  54.7 0.0 copy-start.1
  54.7 0.9 multiply_reduce_fusion
  55.6 0.6 convert_reduce_fusion
  56.3 43.2 %all-reduce = (f32[]{:T(128)}, f32[]{:T(128)}) all-reduce(f32[]{:T(128)} %get-tuple-element.3, f32[]{:T(128)} %get-tuple-element.2), channel_id=1, replica_groups=mesh['lat'=8,'lon'=4] {'lat','lon'}, use_global_device_ids=true, to_apply=%region_2.0 | all-reduce | flops 2 | bytes 16 | tf_op jit(solution)/shard_map/psum | solution.py:76
  100.8 0.1 sqrt_multiply_fusion
  100.9 0.9 broadcast_multiply_fusion.16
  (6 shorter events, 0.0 us)
Async XLA Ops:
  0.6 18.7 %copy-start.4 = (f32[8,16,256]{2,1,0:T(8,128)S(1)}, f32[8,16,256]{2,1,0:T(8,128)}, u32[]{:S(2)}) copy-start(f32[8,16,256]{2,1,0:T(8,128)} %param.6) | copy-start | bytes 393220
  0.6 18.7 %copy-start.3 = (f32[8,16,256]{2,1,0:T(8,128)S(1)}, f32[8,16,256]{2,1,0:T(8,128)}, u32[]{:S(2)}) copy-start(f32[8,16,256]{2,1,0:T(8,128)} %param.7) | copy-start | bytes 393220
  0.7 18.7 %copy-start.2 = (f32[8,16,256]{2,1,0:T(8,128)S(1)}, f32[8,16,256]{2,1,0:T(8,128)}, u32[]{:S(2)}) copy-start(f32[8,16,256]{2,1,0:T(8,128)} %param.8) | copy-start | bytes 393220
  2.7 19.7 %copy-start = (f32[4,8,16,256]{3,2,1,0:T(8,128)S(1)}, f32[4,8,16,256]{3,2,1,0:T(8,128)}, u32[]{:S(2)}) copy-start(f32[4,8,16,256]{3,2,1,0:T(8,128)} %param.5) | copy-start | bytes 1572868
  2.9 12.3 %collective-permute-start = (f32[4,8,16,4]{3,2,1,0:T(8,128)S(1)}, f32[4,8,16,4]{3,2,1,0:T(8,128)S(1)}, u32[]{:S(2)}, u32[]{:S(2)}) collective-permute-start(f32[4,8,16,4]{3,2,1,0:T(8,128)S(1)} %get-tuple-element.58), channel_id=1, source_target_pairs={{0,1},{1,2},{2,3},{3,0},{4,5},{5,6},{6,7},{7,4},{8,9},{9,10},{10,1... | collective-permute-start | bytes 24584 | tf_op jit(solution)/shard_map/ppermute | solution.py:17
  6.0 13.4 %collective-permute-start.1 = (f32[4,8,16,4]{3,2,1,0:T(8,128)S(1)}, f32[4,8,16,4]{3,2,1,0:T(8,128)S(1)}, u32[]{:S(2)}, u32[]{:S(2)}) collective-permute-start(f32[4,8,16,4]{3,2,1,0:T(8,128)S(1)} %get-tuple-element.59), channel_id=1, source_target_pairs={{1,0},{2,1},{3,2},{0,3},{5,4},{6,5},{7,6},{4,7},{9,8},{10,9},{11,1... | collective-permute-start | bytes 24584 | tf_op jit(solution)/shard_map/ppermute | solution.py:18
  19.7 22.8 %collective-permute-start.2 = (f32[4,8,4,264]{3,2,1,0:T(4,128)S(1)}, f32[4,8,4,264]{3,2,1,0:T(4,128)S(1)}, u32[]{:S(2)}, u32[]{:S(2)}) collective-permute-start(f32[4,8,4,264]{3,2,1,0:T(4,128)S(1)} %get-tuple-element.54), channel_id=1, source_target_pairs={{0,4},{4,8},{8,12},{12,16},{16,20},{20,24},{24,28},{1,5},{5,9},{9,... | collective-permute-start | bytes 405512 | tf_op jit(solution)/shard_map/ppermute | solution.py:17
  21.1 21.5 %collective-permute-start.3 = (f32[4,8,4,264]{3,2,1,0:T(4,128)S(1)}, f32[4,8,4,264]{3,2,1,0:T(4,128)S(1)}, u32[]{:S(2)}, u32[]{:S(2)}) collective-permute-start(f32[4,8,4,264]{3,2,1,0:T(4,128)S(1)} %get-tuple-element.55), channel_id=1, source_target_pairs={{4,0},{8,4},{12,8},{16,12},{20,16},{24,20},{28,24},{5,1},{9,5},{13... | collective-permute-start | bytes 405512 | tf_op jit(solution)/shard_map/ppermute | solution.py:18
  22.5 9.4 %collective-permute-start.4 = (f32[4,8,16,4]{3,2,1,0:T(8,128)S(1)}, f32[4,8,16,4]{3,2,1,0:T(8,128)S(1)}, u32[]{:S(2)}, u32[]{:S(2)}) collective-permute-start(f32[4,8,16,4]{3,2,1,0:T(8,128)S(1)} %get-tuple-element.56), channel_id=1, source_target_pairs={{0,1},{1,2},{2,3},{3,0},{4,5},{5,6},{6,7},{7,4},{8,9},{9,10},{10,1... | collective-permute-start | bytes 24584 | tf_op jit(solution)/shard_map/ppermute | solution.py:17
  24.3 14.6 %collective-permute-start.5 = (f32[4,8,16,4]{3,2,1,0:T(8,128)S(1)}, f32[4,8,16,4]{3,2,1,0:T(8,128)S(1)}, u32[]{:S(2)}, u32[]{:S(2)}) collective-permute-start(f32[4,8,16,4]{3,2,1,0:T(8,128)S(1)} %get-tuple-element.57), channel_id=1, source_target_pairs={{1,0},{2,1},{3,2},{0,3},{5,4},{6,5},{7,6},{4,7},{9,8},{10,9},{11,1... | collective-permute-start | bytes 24584 | tf_op jit(solution)/shard_map/ppermute | solution.py:18
  39.2 5.8 %collective-permute-start.6 = (f32[4,8,4,264]{3,2,1,0:T(4,128)S(1)}, f32[4,8,4,264]{3,2,1,0:T(4,128)S(1)}, u32[]{:S(2)}, u32[]{:S(2)}) collective-permute-start(f32[4,8,4,264]{3,2,1,0:T(4,128)S(1)} %get-tuple-element.52), channel_id=1, source_target_pairs={{0,4},{4,8},{8,12},{12,16},{16,20},{20,24},{24,28},{1,5},{5,9},{9,... | collective-permute-start | bytes 405512 | tf_op jit(solution)/shard_map/ppermute | solution.py:17
  41.2 5.5 %collective-permute-start.7 = (f32[4,8,4,264]{3,2,1,0:T(4,128)S(1)}, f32[4,8,4,264]{3,2,1,0:T(4,128)S(1)}, u32[]{:S(2)}, u32[]{:S(2)}) collective-permute-start(f32[4,8,4,264]{3,2,1,0:T(4,128)S(1)} %get-tuple-element.53), channel_id=1, source_target_pairs={{4,0},{8,4},{12,8},{16,12},{20,16},{24,20},{28,24},{5,1},{9,5},{13... | collective-permute-start | bytes 405512 | tf_op jit(solution)/shard_map/ppermute | solution.py:18
  54.7 0.9 copy-start.1
where the time goes:
time: 103 us
  blocking collectives  43.2 us (42%)
  waiting for transfers between devices  25.4 us (25%)
  starting transfers between devices  15.1 us (15%)
  other arithmetic  15 us (15%)
  between operations  3.33 us (3%)
    psum x1, blocking collectives, shards(): lax.psum((jnp.sum(wet * var), jnp.sum(wet)), ('lat', 'lon'))  43.2 us
    ppermute x4, waiting for transfers between devices, with_halo(): after = lax.ppermute(first, axis, down)  12.8 us
    ppermute x4, waiting for transfers between devices, with_halo(): before = lax.ppermute(last, axis, up)  12.6 us
    mul x12, other arithmetic, adjoint_step(): product = weight * masked  9.35 us
    ppermute x4, starting transfers between devices, with_halo(): before = lax.ppermute(last, axis, up)  8.25 us
    ppermute x4, starting transfers between devices, with_halo(): after = lax.ppermute(first, axis, down)  6.81 us
  transfers between devices with their start and end apart: 8, of which 5 were waited for; matrix products, arithmetic and copies ran while one was open for 3% of the time, Pallas kernels for 0%

commit v1 on v0

--- a/solution.py
+++ b/solution.py
@@ -73,7 +73,7 @@
         ]
         field = adjoint_step(field, tensors)
     var = jnp.sum(field * field, axis=0) / SAMPLES
-    wet_sum, wet_count = lax.psum((jnp.sum(wet * var), jnp.sum(wet)), ("lat", "lon"))
+    wet_sum, wet_count = lax.psum(lax.psum((jnp.sum(wet * var), jnp.sum(wet)), "lat"), "lon")
     mean_var = wet_sum / wet_count
     safe = jnp.where(wet > 0, var, 1.0)
     factor = wet * jnp.sqrt(mean_var / (safe + 1e-06))

time: 103 us -> 88.1 us (0.86)
  blocking collectives: 43.2 us -> 27.6 us
    psum x1 -> x2, blocking collectives: 43.2 us -> 27.6 us  [the longest x1 16.6 us: shards(): lax.psum((jnp.sum(wet * var), jnp.sum(wet)), 'lat')]
where the time goes in v1:
time: 88.1 us; the launch traced here: 87.3 us
  blocking collectives  27.6 us (31%)
  waiting for transfers between devices  25.4 us (29%)
  starting transfers between devices  15.1 us (17%)
  other arithmetic  15 us (17%)
  between operations  3.33 us (4%)
    psum x1, blocking collectives, shards(): lax.psum((jnp.sum(wet * var), jnp.sum(wet)), 'lat')  16.6 us
    ppermute x4, waiting for transfers between devices, with_halo(): after = lax.ppermute(first, axis, down)  12.8 us
    ppermute x4, waiting for transfers between devices, with_halo(): before = lax.ppermute(last, axis, up)  12.6 us
    psum x1, blocking collectives, shards(): lax.psum(lax.psum((jnp.sum(wet * var), jnp.sum(wet)), 'lat'), 'lon')  11 us
    mul x12, other arithmetic, adjoint_step(): product = weight * masked  9.35 us
    ppermute x4, starting transfers between devices, with_halo(): before = lax.ppermute(last, axis, up)  8.25 us
    ppermute x4, starting transfers between devices, with_halo(): after = lax.ppermute(first, axis, down)  6.81 us
    another operation x2, other arithmetic, shards(): stacked = jnp.stack([diff_lat, diff_lon, shear, wet], axis=0)  2.04 us
  transfers between devices with their start and end apart: 8, of which 5 were waited for; matrix products, arithmetic and copies ran while one was open for 3% of the time, Pallas kernels for 0%

profile of v1, /device:TPU:0, one launch (start us, length us, event | category | flops | bytes accessed | tf_op | source)
XLA Modules:
  0.0 87.3 jit_solution(17869910768952787258)
XLA Ops:
  0.6 0.0 copy-start.4
  0.6 0.0 copy-start.3
  0.7 0.0 copy-start.2
  0.7 1.0 %convert_bitcast_fusion = f32[1,8,16,256]{3,2,1,0:T(8,128)S(1)} fusion(s32[8,16,256]{2,1,0:T(8,128)} %param.9), kind=kLoop, calls=%fused_computation.101 | loop fusion | flops 32768 | bytes 262144 | tf_op jit(solution)/shard_map/stack | solution.py:65
  1.6 1.1 %pad_maximum_fusion.1 = f32[4,8,16,256]{3,2,1,0:T(8,128)S(1)} fusion(f32[1,8,16,256]{3,2,1,0:T(8,128)S(1)} %convert_bitcast_fusion, f32[1,8,16,256]{3,2,1,0:T(8,128)} %bitcast.53, f32[1,8,16,256]{3,2,1,0:T(8,128)} %bitcast.56, f32[1,8,16,256]{3,2,1,0:T(8,128)} %bitcast.59), kind=kLoop, calls=%fused_computation.57 | loop fusion | flops 393216 | bytes 1048576 | tf_op jit(solution)/shard_map/stack | solution.py:65
  2.7 0.0 copy-start
  2.7 0.1 fusion.7
  2.9 3.1 %collective-permute-start = (f32[4,8,16,4]{3,2,1,0:T(8,128)S(1)}, f32[4,8,16,4]{3,2,1,0:T(8,128)S(1)}, u32[]{:S(2)}, u32[]{:S(2)}) collective-permute-start(f32[4,8,16,4]{3,2,1,0:T(8,128)S(1)} %get-tuple-element.60), channel_id=1, source_target_pairs={{0,1},{1,2},{2,3},{3,0},{4,5},{5,6},{6,7},{7,4},{8,9},{9,10},{10,1... | collective-permute-start | bytes 24584 | tf_op jit(solution)/shard_map/ppermute | solution.py:17
  6.0 2.1 %collective-permute-start.1 = (f32[4,8,16,4]{3,2,1,0:T(8,128)S(1)}, f32[4,8,16,4]{3,2,1,0:T(8,128)S(1)}, u32[]{:S(2)}, u32[]{:S(2)}) collective-permute-start(f32[4,8,16,4]{3,2,1,0:T(8,128)S(1)} %get-tuple-element.61), channel_id=1, source_target_pairs={{1,0},{2,1},{3,2},{0,3},{5,4},{6,5},{7,6},{4,7},{9,8},{10,9},{11,1... | collective-permute-start | bytes 24584 | tf_op jit(solution)/shard_map/ppermute | solution.py:18
  8.0 7.1 %collective-permute-done = f32[4,8,16,4]{3,2,1,0:T(8,128)S(1)} collective-permute-done((f32[4,8,16,4]{3,2,1,0:T(8,128)S(1)}, f32[4,8,16,4]{3,2,1,0:T(8,128)S(1)}, u32[]{:S(2)}, u32[]{:S(2)}) %collective-permute-start) | collective-permute-done | bytes 8224 | tf_op jit(solution)/shard_map/ppermute | solution.py:17
  15.2 4.2 %collective-permute-done.1 = f32[4,8,16,4]{3,2,1,0:T(8,128)S(1)} collective-permute-done((f32[4,8,16,4]{3,2,1,0:T(8,128)S(1)}, f32[4,8,16,4]{3,2,1,0:T(8,128)S(1)}, u32[]{:S(2)}, u32[]{:S(2)}) %collective-permute-start.1) | collective-permute-done | bytes 8224 | tf_op jit(solution)/shard_map/ppermute | solution.py:18
  19.4 0.3 pad_maximum_fusion.10
  19.7 1.4 %collective-permute-start.2 = (f32[4,8,4,264]{3,2,1,0:T(4,128)S(1)}, f32[4,8,4,264]{3,2,1,0:T(4,128)S(1)}, u32[]{:S(2)}, u32[]{:S(2)}) collective-permute-start(f32[4,8,4,264]{3,2,1,0:T(4,128)S(1)} %get-tuple-element.56), channel_id=1, source_target_pairs={{0,4},{4,8},{8,12},{12,16},{16,20},{20,24},{24,28},{1,5},{5,9},{9,... | collective-permute-start | bytes 405512 | tf_op jit(solution)/shard_map/ppermute | solution.py:17
  21.1 1.3 %collective-permute-start.3 = (f32[4,8,4,264]{3,2,1,0:T(4,128)S(1)}, f32[4,8,4,264]{3,2,1,0:T(4,128)S(1)}, u32[]{:S(2)}, u32[]{:S(2)}) collective-permute-start(f32[4,8,4,264]{3,2,1,0:T(4,128)S(1)} %get-tuple-element.57), channel_id=1, source_target_pairs={{4,0},{8,4},{12,8},{16,12},{20,16},{24,20},{28,24},{5,1},{9,5},{13... | collective-permute-start | bytes 405512 | tf_op jit(solution)/shard_map/ppermute | solution.py:18
  22.4 0.1 fusion.6
  22.5 1.7 %collective-permute-start.4 = (f32[4,8,16,4]{3,2,1,0:T(8,128)S(1)}, f32[4,8,16,4]{3,2,1,0:T(8,128)S(1)}, u32[]{:S(2)}, u32[]{:S(2)}) collective-permute-start(f32[4,8,16,4]{3,2,1,0:T(8,128)S(1)} %get-tuple-element.58), channel_id=1, source_target_pairs={{0,1},{1,2},{2,3},{3,0},{4,5},{5,6},{6,7},{7,4},{8,9},{9,10},{10,1... | collective-permute-start | bytes 24584 | tf_op jit(solution)/shard_map/ppermute | solution.py:17
  24.3 2.1 %collective-permute-start.5 = (f32[4,8,16,4]{3,2,1,0:T(8,128)S(1)}, f32[4,8,16,4]{3,2,1,0:T(8,128)S(1)}, u32[]{:S(2)}, u32[]{:S(2)}) collective-permute-start(f32[4,8,16,4]{3,2,1,0:T(8,128)S(1)} %get-tuple-element.59), channel_id=1, source_target_pairs={{1,0},{2,1},{3,2},{0,3},{5,4},{6,5},{7,6},{4,7},{9,8},{10,9},{11,1... | collective-permute-start | bytes 24584 | tf_op jit(solution)/shard_map/ppermute | solution.py:18
  26.4 5.5 %collective-permute-done.4 = f32[4,8,16,4]{3,2,1,0:T(8,128)S(1)} collective-permute-done((f32[4,8,16,4]{3,2,1,0:T(8,128)S(1)}, f32[4,8,16,4]{3,2,1,0:T(8,128)S(1)}, u32[]{:S(2)}, u32[]{:S(2)}) %collective-permute-start.4) | collective-permute-done | bytes 8224 | tf_op jit(solution)/shard_map/ppermute | solution.py:17
  31.9 7.0 %collective-permute-done.5 = f32[4,8,16,4]{3,2,1,0:T(8,128)S(1)} collective-permute-done((f32[4,8,16,4]{3,2,1,0:T(8,128)S(1)}, f32[4,8,16,4]{3,2,1,0:T(8,128)S(1)}, u32[]{:S(2)}, u32[]{:S(2)}) %collective-permute-start.5) | collective-permute-done | bytes 8224 | tf_op jit(solution)/shard_map/ppermute | solution.py:18
  38.9 0.3 pad_maximum_fusion.4
  39.2 2.0 %collective-permute-start.6 = (f32[4,8,4,264]{3,2,1,0:T(4,128)S(1)}, f32[4,8,4,264]{3,2,1,0:T(4,128)S(1)}, u32[]{:S(2)}, u32[]{:S(2)}) collective-permute-start(f32[4,8,4,264]{3,2,1,0:T(4,128)S(1)} %get-tuple-element.54), channel_id=1, source_target_pairs={{0,4},{4,8},{8,12},{12,16},{16,20},{20,24},{24,28},{1,5},{5,9},{9,... | collective-permute-start | bytes 405512 | tf_op jit(solution)/shard_map/ppermute | solution.py:17
  41.2 1.3 %collective-permute-start.7 = (f32[4,8,4,264]{3,2,1,0:T(4,128)S(1)}, f32[4,8,4,264]{3,2,1,0:T(4,128)S(1)}, u32[]{:S(2)}, u32[]{:S(2)}) collective-permute-start(f32[4,8,4,264]{3,2,1,0:T(4,128)S(1)} %get-tuple-element.55), channel_id=1, source_target_pairs={{4,0},{8,4},{12,8},{16,12},{20,16},{24,20},{28,24},{5,1},{9,5},{13... | collective-permute-start | bytes 405512 | tf_op jit(solution)/shard_map/ppermute | solution.py:18
  42.5 0.0 collective-permute-done.2
  42.6 0.5 pad_maximum_fusion
  43.1 0.2 subtract_bitcast_fusion
  43.2 0.4 subtract_bitcast_fusion.1
  43.6 0.4 subtract_bitcast_fusion.2
  44.1 0.4 subtract_bitcast_fusion.3
  44.5 0.1 slice.269
  44.6 0.1 slice.280
  44.8 0.1 slice.291
  44.9 0.1 slice.302
  45.0 1.7 %collective-permute-done.7 = f32[4,8,4,264]{3,2,1,0:T(4,128)S(1)} collective-permute-done((f32[4,8,4,264]{3,2,1,0:T(4,128)S(1)}, f32[4,8,4,264]{3,2,1,0:T(4,128)S(1)}, u32[]{:S(2)}, u32[]{:S(2)}) %collective-permute-start.7) | collective-permute-done | bytes 135200 | tf_op jit(solution)/shard_map/ppermute | solution.py:18
  46.7 0.6 broadcast_multiply_fusion.15
  47.3 0.3 broadcast_multiply_fusion.14
  47.7 2.0 %broadcast_multiply_fusion.11 = (f32[4,8,22,262]{3,2,1,0:T(8,128)S(1)}, f32[4,8,22,262]{3,2,1,0:T(8,128)S(1)}) fusion(f32[8,22,262]{2,1,0:T(8,128)S(1)} %get-tuple-element.41, f32[4,8,24,264]{3,2,1,0:T(8,128)S(1)} %get-tuple-element.53, f32[4,8,24,264]{3,2,1,0:T(8,128)S(1)} %get-tuple-element.52, f32[4,8,24,264]{3,2,1,0:T(8,128)S(1)} %get-tuple-element.51, ...), kind=kLoop, calls=%fused_computation.43 | loop fusion | flops 2028928 | bytes 8669056 | tf_op jit(solution)/shard_map/mul | solution.py:48
  49.7 0.3 broadcast_multiply_fusion.10
  50.0 2.0 %broadcast_multiply_fusion.7 = (f32[4,8,20,260]{3,2,1,0:T(8,128)S(1)}, f32[4,8,20,260]{3,2,1,0:T(8,128)S(1)}) fusion(f32[8,20,260]{2,1,0:T(8,128)S(1)} %get-tuple-element.32, f32[4,8,22,262]{3,2,1,0:T(8,128)S(1)} %get-tuple-element.44, f32[4,8,22,262]{3,2,1,0:T(8,128)S(1)} %get-tuple-element.43, f32[4,8,22,262]{3,2,1,0:T(8,128)S(1)} %get-tuple-element.42, ...), kind=kLoop, calls=%fused_computation.39 | loop fusion | flops 1830400 | bytes 7820800 | tf_op jit(solution)/shard_map/mul | solution.py:48
  52.0 0.3 broadcast_multiply_fusion.6
  52.4 2.0 %broadcast_multiply_fusion.3 = (f32[4,8,18,258]{3,2,1,0:T(8,128)S(1)}, f32[4,8,18,258]{3,2,1,0:T(8,128)S(1)}) fusion(f32[8,18,258]{2,1,0:T(8,128)S(1)} %get-tuple-element.23, f32[4,8,20,260]{3,2,1,0:T(8,128)S(1)} %get-tuple-element.35, f32[4,8,20,260]{3,2,1,0:T(8,128)S(1)} %get-tuple-element.34, f32[4,8,20,260]{3,2,1,0:T(8,128)S(1)} %get-tuple-element.33, ...), kind=kLoop, calls=%fused_computation.35 | loop fusion | flops 1634688 | bytes 6984576 | tf_op jit(solution)/shard_map/mul | solution.py:48
  54.4 0.3 broadcast_multiply_fusion.2
  54.7 0.0 copy-start.1
  54.7 0.9 %multiply_reduce_fusion = (f32[8,16,256]{2,1,0:T(8,128)S(1)}, f32[4,8,16,256]{3,2,1,0:T(8,128)S(1)}) fusion(f32[4,8,18,258]{3,2,1,0:T(8,128)S(1)} %get-tuple-element.26, f32[4,8,18,258]{3,2,1,0:T(8,128)S(1)} %get-tuple-element.25, f32[4,8,18,258]{3,2,1,0:T(8,128)S(1)} %get-tuple-element.24, f32[4,8,18,258]{3,2,1,0:T(8,128)S(1)} %get-tuple-element.10, ...), kind=kLoop, calls=%fused_computation.58 | loop fusion | flops 1409024 | bytes 5505024 | tf_op jit(solution)/shard_map/reduce_sum | solution.py:75
  55.6 0.6 convert_reduce_fusion
  56.3 16.6 %all-reduce = (f32[]{:T(128)}, f32[]{:T(128)}) all-reduce(f32[]{:T(128)} %get-tuple-element.3, f32[]{:T(128)} %get-tuple-element.2), channel_id=1, replica_groups=mesh['lat'=8,'lon'=4] {'lat'}, use_global_device_ids=true, to_apply=%region_2.0 | all-reduce | flops 2 | bytes 16 | tf_op jit(solution)/shard_map/psum | solution.py:76
  72.8 11.0 %all-reduce.1 = (f32[]{:T(128)}, f32[]{:T(128)}) all-reduce(f32[]{:T(128)} %get-tuple-element.4, f32[]{:T(128)} %get-tuple-element.5), channel_id=1, replica_groups=mesh['lat'=8,'lon'=4] {'lon'}, use_global_device_ids=true, to_apply=%region_3.0 | all-reduce | flops 2 | bytes 16 | tf_op jit(solution)/shard_map/psum | solution.py:76
  85.2 0.1 sqrt_multiply_fusion
  85.3 0.9 broadcast_multiply_fusion.16
  (7 shorter events, 0.0 us)
Async XLA Ops:
  0.6 18.7 %copy-start.4 = (f32[8,16,256]{2,1,0:T(8,128)S(1)}, f32[8,16,256]{2,1,0:T(8,128)}, u32[]{:S(2)}) copy-start(f32[8,16,256]{2,1,0:T(8,128)} %param.6) | copy-start | bytes 393220
  0.6 18.7 %copy-start.3 = (f32[8,16,256]{2,1,0:T(8,128)S(1)}, f32[8,16,256]{2,1,0:T(8,128)}, u32[]{:S(2)}) copy-start(f32[8,16,256]{2,1,0:T(8,128)} %param.7) | copy-start | bytes 393220
  0.7 18.7 %copy-start.2 = (f32[8,16,256]{2,1,0:T(8,128)S(1)}, f32[8,16,256]{2,1,0:T(8,128)}, u32[]{:S(2)}) copy-start(f32[8,16,256]{2,1,0:T(8,128)} %param.8) | copy-start | bytes 393220
  2.7 19.7 %copy-start = (f32[4,8,16,256]{3,2,1,0:T(8,128)S(1)}, f32[4,8,16,256]{3,2,1,0:T(8,128)}, u32[]{:S(2)}) copy-start(f32[4,8,16,256]{3,2,1,0:T(8,128)} %param.5) | copy-start | bytes 1572868
  2.9 12.3 %collective-permute-start = (f32[4,8,16,4]{3,2,1,0:T(8,128)S(1)}, f32[4,8,16,4]{3,2,1,0:T(8,128)S(1)}, u32[]{:S(2)}, u32[]{:S(2)}) collective-permute-start(f32[4,8,16,4]{3,2,1,0:T(8,128)S(1)} %get-tuple-element.60), channel_id=1, source_target_pairs={{0,1},{1,2},{2,3},{3,0},{4,5},{5,6},{6,7},{7,4},{8,9},{9,10},{10,1... | collective-permute-start | bytes 24584 | tf_op jit(solution)/shard_map/ppermute | solution.py:17
  6.0 13.4 %collective-permute-start.1 = (f32[4,8,16,4]{3,2,1,0:T(8,128)S(1)}, f32[4,8,16,4]{3,2,1,0:T(8,128)S(1)}, u32[]{:S(2)}, u32[]{:S(2)}) collective-permute-start(f32[4,8,16,4]{3,2,1,0:T(8,128)S(1)} %get-tuple-element.61), channel_id=1, source_target_pairs={{1,0},{2,1},{3,2},{0,3},{5,4},{6,5},{7,6},{4,7},{9,8},{10,9},{11,1... | collective-permute-start | bytes 24584 | tf_op jit(solution)/shard_map/ppermute | solution.py:18
  19.7 22.8 %collective-permute-start.2 = (f32[4,8,4,264]{3,2,1,0:T(4,128)S(1)}, f32[4,8,4,264]{3,2,1,0:T(4,128)S(1)}, u32[]{:S(2)}, u32[]{:S(2)}) collective-permute-start(f32[4,8,4,264]{3,2,1,0:T(4,128)S(1)} %get-tuple-element.56), channel_id=1, source_target_pairs={{0,4},{4,8},{8,12},{12,16},{16,20},{20,24},{24,28},{1,5},{5,9},{9,... | collective-permute-start | bytes 405512 | tf_op jit(solution)/shard_map/ppermute | solution.py:17
  21.1 21.5 %collective-permute-start.3 = (f32[4,8,4,264]{3,2,1,0:T(4,128)S(1)}, f32[4,8,4,264]{3,2,1,0:T(4,128)S(1)}, u32[]{:S(2)}, u32[]{:S(2)}) collective-permute-start(f32[4,8,4,264]{3,2,1,0:T(4,128)S(1)} %get-tuple-element.57), channel_id=1, source_target_pairs={{4,0},{8,4},{12,8},{16,12},{20,16},{24,20},{28,24},{5,1},{9,5},{13... | collective-permute-start | bytes 405512 | tf_op jit(solution)/shard_map/ppermute | solution.py:18
  22.5 9.4 %collective-permute-start.4 = (f32[4,8,16,4]{3,2,1,0:T(8,128)S(1)}, f32[4,8,16,4]{3,2,1,0:T(8,128)S(1)}, u32[]{:S(2)}, u32[]{:S(2)}) collective-permute-start(f32[4,8,16,4]{3,2,1,0:T(8,128)S(1)} %get-tuple-element.58), channel_id=1, source_target_pairs={{0,1},{1,2},{2,3},{3,0},{4,5},{5,6},{6,7},{7,4},{8,9},{9,10},{10,1... | collective-permute-start | bytes 24584 | tf_op jit(solution)/shard_map/ppermute | solution.py:17
  24.3 14.6 %collective-permute-start.5 = (f32[4,8,16,4]{3,2,1,0:T(8,128)S(1)}, f32[4,8,16,4]{3,2,1,0:T(8,128)S(1)}, u32[]{:S(2)}, u32[]{:S(2)}) collective-permute-start(f32[4,8,16,4]{3,2,1,0:T(8,128)S(1)} %get-tuple-element.59), channel_id=1, source_target_pairs={{1,0},{2,1},{3,2},{0,3},{5,4},{6,5},{7,6},{4,7},{9,8},{10,9},{11,1... | collective-permute-start | bytes 24584 | tf_op jit(solution)/shard_map/ppermute | solution.py:18
  39.2 5.8 %collective-permute-start.6 = (f32[4,8,4,264]{3,2,1,0:T(4,128)S(1)}, f32[4,8,4,264]{3,2,1,0:T(4,128)S(1)}, u32[]{:S(2)}, u32[]{:S(2)}) collective-permute-start(f32[4,8,4,264]{3,2,1,0:T(4,128)S(1)} %get-tuple-element.54), channel_id=1, source_target_pairs={{0,4},{4,8},{8,12},{12,16},{16,20},{20,24},{24,28},{1,5},{5,9},{9,... | collective-permute-start | bytes 405512 | tf_op jit(solution)/shard_map/ppermute | solution.py:17
  41.2 5.5 %collective-permute-start.7 = (f32[4,8,4,264]{3,2,1,0:T(4,128)S(1)}, f32[4,8,4,264]{3,2,1,0:T(4,128)S(1)}, u32[]{:S(2)}, u32[]{:S(2)}) collective-permute-start(f32[4,8,4,264]{3,2,1,0:T(4,128)S(1)} %get-tuple-element.55), channel_id=1, source_target_pairs={{4,0},{8,4},{12,8},{16,12},{20,16},{24,20},{28,24},{5,1},{9,5},{13... | collective-permute-start | bytes 405512 | tf_op jit(solution)/shard_map/ppermute | solution.py:18
  54.7 0.9 %copy-start.1 = (s32[8,16,256]{2,1,0:T(8,128)S(1)}, s32[8,16,256]{2,1,0:T(8,128)}, u32[]{:S(2)}) copy-start(s32[8,16,256]{2,1,0:T(8,128)} %param.9) | copy-start | bytes 393220
